TPU v7x, 256 devices: a whole 4x4x8 slice. The times are simulated.
256 devices in a mesh: kv: 2 (over y_hi), blk: 128 (over x, y_lo, z, core).
Axes of the slice: x: 4, y: 4 (y_hi: 2, y_lo: 2; y = y_hi * 2 + y_lo), z: 8, core: 2. Of those that a mesh axis runs over, the one named last changes fastest.
Arguments:
- hidden_in: bfloat16 [65536, 1280], P('blk'), may hold values from -6 to 6
- w_query: bfloat16 [1280, 1280], P(None, 'kv'), may hold values from -0.15625 to 0.15625
- w_key: bfloat16 [1280, 1280], P(None, 'kv'), may hold values from -0.15625 to 0.15625
- w_value: bfloat16 [1280, 1280], P(None, 'kv'), may hold values from -0.15625 to 0.15625
- w_out: bfloat16 [1280, 1280], P('kv'), may hold values from -0.15625 to 0.15625
- head_gain: float32 [1280], P('kv'), may hold values from 1 to 2.5
- eigen_rate: float32 [1280], replicated, may hold values from 0.15 to 0.6
- pool_keys: bfloat16 [512, 256, 1280], P('blk', None, 'kv'), may hold values from -2 to 2
- pool_values: bfloat16 [512, 256, 1280], P('blk', None, 'kv'), may hold values from -6 to 6
- req_len: int32 [128], P('blk'), may hold values from 1 to 512, as said below
- prefix_len: int32 [128], P('blk'), may hold values from 0 to 4, as said below
- prefix_pages: int32 [128, 4], replicated, may hold values from 0 to 511, as said below
- placement: int32 [256], replicated, may hold values from 0 to 255, as said below
Outputs:
- layer_out: bfloat16 [65536, 1280], P('blk')
- new_keys: bfloat16 [256, 256, 1280], P('blk', None, 'kv')
- new_values: bfloat16 [256, 256, 1280], P('blk', None, 'kv')
Inputs may be any that keep to these rules, and one draw needn't show every extreme that they name: `req_len`: some request has all 512 tokens live. `prefix_len`: some request has 4 cached pages. Page prefix_pages[r, s] lies among pages h * 4 to (h + 1) * 4 - 1 with h = (r + 1 + s * 32) mod 128, for every slot s. Each page once; placement[b] lies among pages e * 2 to (e + 1) * 2 - 1 with e = (b // 2 + (2 * (b mod 2) + 1) * 32) mod 128.
All inputs are finite; a program needn't handle non-finite values.
Results may differ from a plain program's by a relative error of at most 0.0067.
Values may be sent and summed in bfloat16 or wider, within the bound.
A program may use at most 128 MiB of HBM per device.

v0:
```python
import math
import jax
import jax.numpy as jnp
from jax import lax
from jax.sharding import PartitionSpec as P

HD = 64
PAGE = 256
PMAX = 4
epsilon = 1e-06


def from_behind(block, axis, distance):
    devices = range(lax.axis_size(axis))
    route = [((i - distance) % len(devices), i) for i in devices]
    return lax.ppermute(block, axis, route)


def rms_scale(values):
    return values * lax.rsqrt(jnp.mean(values * values, axis=-1, keepdims=True) + epsilon)


def head_normed(projected, head_gain):
    count = projected.shape[0]
    split_heads = projected.reshape(count, -1, HD)
    return (rms_scale(split_heads).reshape(count, -1) * head_gain).astype(jnp.bfloat16)


def attend(query_heads, key_rows, value_rows, visible):
    key_heads = key_rows.reshape(key_rows.shape[0], -1, HD)
    value_heads = value_rows.reshape(value_rows.shape[0], -1, HD)
    scores = jnp.einsum(
        "qhd,khd->hqk", query_heads, key_heads, preferred_element_type=jnp.float32
    ) / math.sqrt(HD)
    weights = jnp.where(visible, jnp.exp(scores), 0.0)
    totals = jnp.sum(weights, axis=-1)
    mixed = jnp.einsum(
        "hqk,khd->qhd",
        weights.astype(jnp.bfloat16),
        value_heads,
        preferred_element_type=jnp.float32,
    )
    return (totals, mixed)


def fetch_page(pool_keys, pool_values, prefix_pages, slot_index):
    devices = lax.axis_size("blk")
    here = lax.axis_index("blk")
    offset = slot_index * devices // PMAX + 1
    asker = (here - offset) % devices
    local = prefix_pages[asker, slot_index] % pool_keys.shape[0]
    send_keys = lax.dynamic_index_in_dim(pool_keys, local, 0, keepdims=False)
    send_values = lax.dynamic_index_in_dim(pool_values, local, 0, keepdims=False)
    return from_behind((send_keys, send_values), "blk", devices - offset)


def relay(key_rows, value_rows, placement):
    devices = lax.axis_size("blk")
    here = lax.axis_index("blk")
    blocks = key_rows.shape[0] // PAGE
    width = key_rows.shape[1]
    key_pages = key_rows.reshape(blocks, PAGE, width)
    value_pages = value_rows.reshape(blocks, PAGE, width)
    key_out = jnp.zeros_like(key_pages)
    value_out = jnp.zeros_like(value_pages)
    for block_index in range(blocks):
        offset = (2 * block_index + 1) * devices // (2 * blocks)
        key_recv, value_recv = from_behind(
            (key_pages[block_index], value_pages[block_index]), "blk", offset
        )
        source = (here - offset) % devices
        target = placement[source * blocks + block_index] % blocks
        key_out = lax.dynamic_update_index_in_dim(key_out, key_recv, target, 0)
        value_out = lax.dynamic_update_index_in_dim(value_out, value_recv, target, 0)
    return (key_out, value_out)


def body(
    hidden_in,
    w_query,
    w_key,
    w_value,
    w_out,
    head_gain,
    eigen_rate,
    pool_keys,
    pool_values,
    req_len,
    prefix_len,
    prefix_pages,
    placement,
):
    tokens_here = hidden_in.shape[0]
    width_half = w_query.shape[1]
    heads_here = width_half // HD
    hidden_f = hidden_in.astype(jnp.float32)
    row_scale = lax.rsqrt(jnp.mean(hidden_f * hidden_f, axis=-1, keepdims=True) + epsilon)
    anchor = hidden_f * row_scale
    queries = head_normed(
        jnp.dot(hidden_in, w_query, preferred_element_type=jnp.float32), head_gain
    )
    key_rows = head_normed(jnp.dot(hidden_in, w_key, preferred_element_type=jnp.float32), head_gain)
    value_rows = (
        jnp.dot(hidden_in, w_value, preferred_element_type=jnp.float32) * row_scale
    ).astype(jnp.bfloat16)
    live_count = req_len[0]
    depth = prefix_len[0]
    query_heads = queries.reshape(tokens_here, heads_here, HD)
    row_index = jnp.arange(tokens_here, dtype=jnp.int32)[:, None]
    col_index = jnp.arange(tokens_here, dtype=jnp.int32)[None, :]
    own_visible = ((col_index <= row_index) & (col_index < live_count))[None]
    totals, mixed = attend(query_heads, key_rows, value_rows, own_visible)
    fetched_keys = []
    fetched_values = []
    for slot_index in range(PMAX):
        page_keys, page_values = fetch_page(pool_keys, pool_values, prefix_pages, slot_index)
        fetched_keys.append(page_keys)
        fetched_values.append(page_values)
    cached_keys = jnp.concatenate(fetched_keys, axis=0)
    cached_values = jnp.concatenate(fetched_values, axis=0)
    page_number = jnp.arange(cached_keys.shape[0], dtype=jnp.int32) // PAGE
    cached_visible = (page_number < depth)[None, None, :]
    more_totals, more_mixed = attend(query_heads, cached_keys, cached_values, cached_visible)
    totals = totals + more_totals
    mixed = mixed + more_mixed
    attended = (mixed / totals.T[:, :, None]).astype(jnp.bfloat16).reshape(tokens_here, width_half)
    partial_branch = jnp.dot(attended, w_out, preferred_element_type=jnp.float32)
    branch = lax.psum(partial_branch, "kv")
    updated = anchor + eigen_rate * (rms_scale(branch) - anchor)
    layer_out = rms_scale(updated).astype(jnp.bfloat16)
    new_keys, new_values = relay(key_rows, value_rows, placement)
    return (layer_out, new_keys, new_values)


def solution(mesh):
    in_specs = (
        P("blk", None),
        P(None, "kv"),
        P(None, "kv"),
        P(None, "kv"),
        P("kv", None),
        P("kv"),
        P(),
        P("blk", None, "kv"),
        P("blk", None, "kv"),
        P("blk"),
        P("blk"),
        P(),
        P(),
    )
    out_specs = (P("blk", None), P("blk", None, "kv"), P("blk", None, "kv"))
    return jax.shard_map(body, mesh=mesh, in_specs=in_specs, out_specs=out_specs, check_vma=False)
```

profile of v0, /device:TPU:1, one launch (start us, length us, event | category | flops | bytes accessed | tf_op | source)
XLA Modules:
  0.0 205.1 jit_solution(14092505884325169063)
XLA Ops:
  16.5 2.5 %dynamic-slice_bitcast_fusion.3 = (bf16[256,640]{1,0:T(8,128)(2,1)}, bf16[256,640]{1,0:T(8,128)(2,1)}, bf16[256,640]{1,0:T(8,128)(2,1)}, bf16[256,640]{1,0:T(8,128)(2,1)}) fusion(bf16[4,256,640]{2,1,0:T(8,128)(2,1)} %param.20, s32[]{:T(128)S(6)} %select_n.116, s32[]{:T(128)S(6)} %select_n.120, s32[]{:T(128)S(6)} %select_n.128, s32[]{:T(128)S(6)} %select_n.124), kind=kLoop, calls=%fused_computation.39 | loop fusion | bytes 2621456 | tf_op jit(solution)/shard_map/jit(dynamic_index_in_dim)/squeeze | solution.py:52
  19.0 3.2 %collective-permute-start.4 = (bf16[256,640]{1,0:T(8,128)(2,1)}, bf16[256,640]{1,0:T(8,128)(2,1)S(1)}, u32[]{:S(2)}, u32[]{:S(2)}) collective-permute-start(bf16[256,640]{1,0:T(8,128)(2,1)} %get-tuple-element.3), channel_id=1, source_target_pairs={{1,0},{2,1},{3,2},{4,3},{5,4},{6,5},{7,6},{8,7},{9,8},{10,9},{11,1... | collective-permute-start | bytes 983048 | tf_op jit(solution)/shard_map/ppermute | solution.py:16
  22.3 7.2 %collective-permute-start.5 = (bf16[256,640]{1,0:T(8,128)(2,1)}, bf16[256,640]{1,0:T(8,128)(2,1)}, u32[]{:S(2)}, u32[]{:S(2)}) collective-permute-start(bf16[256,640]{1,0:T(8,128)(2,1)} %get-tuple-element.4), channel_id=1, source_target_pairs={{33,0},{34,1},{35,2},{36,3},{37,4},{38,5},{39,6},{40,7},{41,8},{42... | collective-permute-start | bytes 983048 | tf_op jit(solution)/shard_map/ppermute | solution.py:16
  35.0 2.2 %copy.21 = bf16[512,640]{0,1:T(8,128)(2,1)} copy(bf16[512,640]{1,0:T(8,128)(2,1)} %fusion.22) | data formatting | bytes 1310720 | tf_op jit(solution)/shard_map/convert_element_type | solution.py:105
  37.2 2.7 %fusion.38 = (f32[512,640]{1,0:T(8,128)}, f32[512,640]{1,0:T(8,128)}) fusion(bf16[512,1280]{1,0:T(8,128)(2,1)S(1)} %copy-done.3, bf16[1280,640]{1,0:T(8,128)(2,1)S(1)} %copy-done), kind=kOutput, calls=%fused_computation.71 | convolution fusion | flops 839188480 | bytes 5570560 | tf_op jit(solution)/shard_map/dot_general | solution.py:100
  43.4 4.1 %fusion.37 = (f32[512,640]{1,0:T(8,128)}, f32[512,640]{1,0:T(8,128)}) fusion(bf16[512,1280]{1,0:T(8,128)(2,1)S(1)} %copy-done.3, bf16[1280,640]{1,0:T(8,128)(2,1)} %param.15), kind=kOutput, calls=%fused_computation.70 | convolution fusion | flops 839188480 | bytes 5570560 | tf_op jit(solution)/shard_map/dot_general | solution.py:102
  51.0 2.8 %multiply_convert_fusion.1 = (bf16[512,640]{1,0:T(8,128)(2,1)S(1)}, bf16[512,640]{1,0:T(8,128)(2,1)S(1)}) fusion(f32[512,640]{1,0:T(8,128)} %get-tuple-element.24, f32[512,640]{1,0:T(8,128)} %copy.26, f32[640]{0:T(1024)S(1)} %copy-done.15, f32[512,640]{1,0:T(8,128)} %get-tuple-element.26, f32[512,640]{1,0:T(8,128)} %copy.23), kind=kLoop, calls=%fused_computation.28 | loop fusion | flops 1966080 | bytes 6556160 | tf_op jit(solution)/shard_map/convert_element_type | solution.py:26
  56.0 4.7 %fusion.5 = (f32[10,512]{1,0:T(8,128)}, f32[10,512,512]{1,2,0:T(8,128)S(1)}) fusion(pred[512,512]{0,1:T(8,128)(4,1)S(1)} %fusion.23, bf16[512,10,64]{0,2,1:T(8,128)(2,1)} %bitcast.71, bf16[512,10,64]{0,2,1:T(8,128)(2,1)} %bitcast.73), kind=kOutput, calls=%fused_computation.6 | convolution fusion | flops 343403520 | bytes 12079104 | tf_op jit(solution)/shard_map/qhd,khd->hqk/dot_general | solution.py:32
  60.7 2.8 %collective-permute-start.1 = (bf16[256,640]{1,0:T(8,128)(2,1)}, bf16[256,640]{1,0:T(8,128)(2,1)}, u32[]{:S(2)}, u32[]{:S(2)}) collective-permute-start(bf16[256,640]{1,0:T(8,128)(2,1)} %get-tuple-element.8), channel_id=1, source_target_pairs={{33,0},{34,1},{35,2},{36,3},{37,4},{38,5},{39,6},{40,7},{41,8},{42... | collective-permute-start | bytes 983048 | tf_op jit(solution)/shard_map/ppermute | solution.py:16
  64.4 2.7 %collective-permute-start.2 = (bf16[256,640]{1,0:T(8,128)(2,1)S(1)}, bf16[256,640]{1,0:T(8,128)(2,1)}, u32[]{:S(2)}, u32[]{:S(2)}) collective-permute-start(bf16[256,640]{1,0:T(8,128)(2,1)S(1)} %copy-done.12), channel_id=1, source_target_pairs={{65,0},{66,1},{67,2},{68,3},{69,4},{70,5},{71,6},{72,7},{73,8},{74... | collective-permute-start | bytes 983048 | tf_op jit(solution)/shard_map/ppermute | solution.py:16
  67.0 2.9 %fusion.7 = f32[10,64,512]{2,1,0:T(8,128)} fusion(bf16[512,10,64]{0,2,1:T(8,128)(2,1)S(1)} %bitcast.68, f32[10,512,512]{1,2,0:T(8,128)S(1)} %get-tuple-element.28, pred[512,512]{0,1:T(8,128)(4,1)S(1)} %fusion.23), kind=kOutput, calls=%fused_computation.8 | convolution fusion | flops 343408640 | bytes 12713984 | tf_op jit(solution)/shard_map/hqk,khd->qhd/dot_general | solution.py:37
  70.6 2.4 %pad_maximum_fusion.1 = bf16[1024,640]{1,0:T(8,128)(2,1)} fusion(bf16[256,640]{1,0:T(8,128)(2,1)} %collective-permute-done.7, bf16[256,640]{1,0:T(8,128)(2,1)} %collective-permute-done.6, bf16[256,640]{1,0:T(8,128)(2,1)} %collective-permute-done.5, bf16[256,640]{1,0:T(8,128)(2,1)S(1)} %collective-permute-done.4), kind=kLoop, calls=%fused_computation.26 | loop fusion | flops 5242880 | bytes 2621440 | tf_op jit(solution)/shard_map/concatenate | solution.py:119
  73.0 2.5 %copy.30 = bf16[1024,640]{0,1:T(8,128)(2,1)} copy(bf16[1024,640]{1,0:T(8,128)(2,1)} %pad_maximum_fusion.1) | data formatting | bytes 2621440 | tf_op jit(solution)/shard_map/concatenate | solution.py:119
  75.5 3.6 %collective-permute-done.2 = bf16[256,640]{1,0:T(8,128)(2,1)} collective-permute-done((bf16[256,640]{1,0:T(8,128)(2,1)S(1)}, bf16[256,640]{1,0:T(8,128)(2,1)}, u32[]{:S(2)}, u32[]{:S(2)}) %collective-permute-start.2) | collective-permute-done | bytes 327712 | tf_op jit(solution)/shard_map/ppermute | solution.py:16
  79.1 2.5 %pad_maximum_fusion = bf16[1024,640]{1,0:T(8,128)(2,1)} fusion(bf16[256,640]{1,0:T(8,128)(2,1)} %collective-permute-done.3, bf16[256,640]{1,0:T(8,128)(2,1)} %collective-permute-done.2, bf16[256,640]{1,0:T(8,128)(2,1)} %collective-permute-done.1, bf16[256,640]{1,0:T(8,128)(2,1)} %collective-permute-done), kind=kLoop, calls=%fused_computation.25 | loop fusion | flops 5242880 | bytes 2621440 | tf_op jit(solution)/shard_map/concatenate | solution.py:120
  81.6 2.6 %copy.29 = bf16[1024,640]{0,1:T(8,128)(2,1)} copy(bf16[1024,640]{1,0:T(8,128)(2,1)} %pad_maximum_fusion) | data formatting | bytes 2621440 | tf_op jit(solution)/shard_map/concatenate | solution.py:120
  84.2 10.9 %fusion = (f32[10,512]{1,0:T(8,128)S(1)}, f32[10,512,1024]{2,1,0:T(8,128)}) fusion(pred[1024]{0:T(1024)(128)(4,1)S(1)} %fusion.26, bf16[512,10,64]{0,2,1:T(8,128)(2,1)S(1)} %bitcast.72, bf16[1024,10,64]{0,2,1:T(8,128)(2,1)} %bitcast.69), kind=kOutput, calls=%fused_computation.1 | convolution fusion | flops 686812160 | bytes 22959104 | tf_op jit(solution)/shard_map/qhd,khd->hqk/dot_general | solution.py:32
  95.1 9.0 %divide_convert_fusion = bf16[512,10,64]{0,2,1:T(8,128)(2,1)S(1)} fusion(f32[10,64,512]{2,1,0:T(8,128)S(1)} %copy-done.6, bf16[1024,10,64]{0,2,1:T(8,128)(2,1)S(1)} %bitcast.70, f32[10,512,1024]{2,1,0:T(8,128)} %get-tuple-element.30, pred[1024]{0:T(1024)(128)(4,1)S(1)} %fusion.26, f32[512,10]{0,1:T(8,128)S(1)} %add_bitcast_fusion), kind=kOutput, calls=%fused_computation.27 | convolution fusion | flops 687800320 | bytes 24269824 | tf_op jit(solution)/shard_map/hqk,khd->qhd/dot_general | solution.py:37
  104.2 2.7 %fusion.39 = f32[512,1280]{1,0:T(8,128)} fusion(bf16[512,640]{0,1:T(8,128)(2,1)S(1)} %bitcast.74, bf16[640,1280]{1,0:T(8,128)(2,1)S(1)} %copy-done.18), kind=kOutput, calls=%fused_computation.72 | convolution fusion | flops 838860800 | bytes 4915200 | tf_op jit(solution)/shard_map/dot_general | solution.py:127
  109.8 3.1 %collective-permute-start.8 = (bf16[256,640]{1,0:T(8,128)(2,1)}, bf16[256,640]{1,0:T(8,128)(2,1)}, u32[]{:S(2)}, u32[]{:S(2)}) collective-permute-start(bf16[256,640]{1,0:T(8,128)(2,1)} %get-tuple-element.14), channel_id=1, source_target_pairs={{96,0},{97,1},{98,2},{99,3},{100,4},{101,5},{102,6},{103,7},{104,8... | collective-permute-start | bytes 983048 | tf_op jit(solution)/shard_map/ppermute | solution.py:16
  119.5 2.1 %collective-permute-done.8 = bf16[256,640]{1,0:T(8,128)(2,1)} collective-permute-done((bf16[256,640]{1,0:T(8,128)(2,1)}, bf16[256,640]{1,0:T(8,128)(2,1)}, u32[]{:S(2)}, u32[]{:S(2)}) %collective-permute-start.8) | collective-permute-done | bytes 327712 | tf_op jit(solution)/shard_map/ppermute | solution.py:16
  123.7 4.0 %collective-permute-done.9 = bf16[256,640]{1,0:T(8,128)(2,1)} collective-permute-done((bf16[256,640]{1,0:T(8,128)(2,1)S(1)}, bf16[256,640]{1,0:T(8,128)(2,1)}, u32[]{:S(2)}, u32[]{:S(2)}) %collective-permute-start.9) | collective-permute-done | bytes 327712 | tf_op jit(solution)/shard_map/ppermute | solution.py:16
  129.6 63.5 %all-reduce.2.cloned.1.call-done = f32[512,1280]{1,0:T(8,128)} async-done(((f32[512,1280]{1,0:T(8,128)}), f32[512,1280]{1,0:T(8,128)}) %all-reduce.2.cloned.1.call-update) | async-done | bytes 2621456 | tf_op jit(solution)/shard_map/psum | solution.py:128
  193.0 2.1 %multiply_reduce_fusion.1 = f32[512]{0:T(512)S(1)} fusion(f32[512,1280]{1,0:T(8,128)} %all-reduce.2.cloned.1.call-done), kind=kLoop, calls=%fused_computation.20 | loop fusion | flops 1310208 | bytes 2623488 | tf_op jit(solution)/shard_map/reduce_sum | solution.py:20
  (90 shorter events, 28.8 us)
Async XLA Ops:
  7.2 30.0 %copy-start = (bf16[1280,640]{1,0:T(8,128)(2,1)S(1)}, bf16[1280,640]{1,0:T(8,128)(2,1)}, u32[]{:S(2)}) copy-start(bf16[1280,640]{1,0:T(8,128)(2,1)} %param.14) | copy-start | bytes 4915204
  7.2 185.9 %all-reduce.2.cloned.1.call-start = ((), (), s32[]{:S(2)}) async-start(), calls=%async_computation | async-start | bytes 5242880 | tf_op jit(solution)/shard_map/psum | solution.py:128
  16.5 14.2 %copy-start.8 = (bf16[4,256,640]{2,1,0:T(8,128)(2,1)S(1)}, bf16[4,256,640]{2,1,0:T(8,128)(2,1)}, u32[]{:S(2)}) copy-start(bf16[4,256,640]{2,1,0:T(8,128)(2,1)} %param.21) | copy-start | bytes 3932164
  19.0 13.5 %copy-start.3 = (bf16[512,1280]{1,0:T(8,128)(2,1)S(1)}, bf16[512,1280]{1,0:T(8,128)(2,1)}, u32[]{:S(2)}) copy-start(bf16[512,1280]{1,0:T(8,128)(2,1)} %param.13) | copy-start | bytes 3932164
  19.0 41.7 %collective-permute-start.4 = (bf16[256,640]{1,0:T(8,128)(2,1)}, bf16[256,640]{1,0:T(8,128)(2,1)S(1)}, u32[]{:S(2)}, u32[]{:S(2)}) collective-permute-start(bf16[256,640]{1,0:T(8,128)(2,1)} %get-tuple-element.3), channel_id=1, source_target_pairs={{1,0},{2,1},{3,2},{4,3},{5,4},{6,5},{7,6},{8,7},{9,8},{10,9},{11,1... | collective-permute-start | bytes 983048 | tf_op jit(solution)/shard_map/ppermute | solution.py:16
  22.3 41.3 %collective-permute-start.5 = (bf16[256,640]{1,0:T(8,128)(2,1)}, bf16[256,640]{1,0:T(8,128)(2,1)}, u32[]{:S(2)}, u32[]{:S(2)}) collective-permute-start(bf16[256,640]{1,0:T(8,128)(2,1)} %get-tuple-element.4), channel_id=1, source_target_pairs={{33,0},{34,1},{35,2},{36,3},{37,4},{38,5},{39,6},{40,7},{41,8},{42... | collective-permute-start | bytes 983048 | tf_op jit(solution)/shard_map/ppermute | solution.py:16
  29.5 34.9 %collective-permute-start.7 = (bf16[256,640]{1,0:T(8,128)(2,1)}, bf16[256,640]{1,0:T(8,128)(2,1)}, u32[]{:S(2)}, u32[]{:S(2)}) collective-permute-start(bf16[256,640]{1,0:T(8,128)(2,1)} %get-tuple-element.5), channel_id=1, source_target_pairs={{97,0},{98,1},{99,2},{100,3},{101,4},{102,5},{103,6},{104,7},{105,... | collective-permute-start | bytes 983048 | tf_op jit(solution)/shard_map/ppermute | solution.py:16
  30.4 40.2 %collective-permute-start.6 = (bf16[256,640]{1,0:T(8,128)(2,1)}, bf16[256,640]{1,0:T(8,128)(2,1)}, u32[]{:S(2)}, u32[]{:S(2)}) collective-permute-start(bf16[256,640]{1,0:T(8,128)(2,1)} %get-tuple-element.6), channel_id=1, source_target_pairs={{65,0},{66,1},{67,2},{68,3},{69,4},{70,5},{71,6},{72,7},{73,8},{74... | collective-permute-start | bytes 983048 | tf_op jit(solution)/shard_map/ppermute | solution.py:16
  31.8 43.7 %collective-permute-start = (bf16[256,640]{1,0:T(8,128)(2,1)}, bf16[256,640]{1,0:T(8,128)(2,1)}, u32[]{:S(2)}, u32[]{:S(2)}) collective-permute-start(bf16[256,640]{1,0:T(8,128)(2,1)} %get-tuple-element.7), channel_id=1, source_target_pairs={{1,0},{2,1},{3,2},{4,3},{5,4},{6,5},{7,6},{8,7},{9,8},{10,9},{11,1... | collective-permute-start | bytes 983048 | tf_op jit(solution)/shard_map/ppermute | solution.py:16
  56.0 8.3 %copy-start.12 = (bf16[256,640]{1,0:T(8,128)(2,1)S(1)}, bf16[256,640]{1,0:T(8,128)(2,1)}, u32[]{:S(2)}) copy-start(bf16[256,640]{1,0:T(8,128)(2,1)} %get-tuple-element.10) | copy-start | bytes 983044
  56.0 11.0 %copy-start.4 = (bf16[512,640]{0,1:T(8,128)(2,1)S(1)}, bf16[512,640]{0,1:T(8,128)(2,1)}, u32[]{:S(2)}) copy-start(bf16[512,640]{0,1:T(8,128)(2,1)} %copy.21) | copy-start | bytes 1966084
  60.7 14.7 %collective-permute-start.1 = (bf16[256,640]{1,0:T(8,128)(2,1)}, bf16[256,640]{1,0:T(8,128)(2,1)}, u32[]{:S(2)}, u32[]{:S(2)}) collective-permute-start(bf16[256,640]{1,0:T(8,128)(2,1)} %get-tuple-element.8), channel_id=1, source_target_pairs={{33,0},{34,1},{35,2},{36,3},{37,4},{38,5},{39,6},{40,7},{41,8},{42... | collective-permute-start | bytes 983048 | tf_op jit(solution)/shard_map/ppermute | solution.py:16
  63.6 11.9 %collective-permute-start.3 = (bf16[256,640]{1,0:T(8,128)(2,1)}, bf16[256,640]{1,0:T(8,128)(2,1)}, u32[]{:S(2)}, u32[]{:S(2)}) collective-permute-start(bf16[256,640]{1,0:T(8,128)(2,1)} %get-tuple-element.9), channel_id=1, source_target_pairs={{97,0},{98,1},{99,2},{100,3},{101,4},{102,5},{103,6},{104,7},{105,... | collective-permute-start | bytes 983048 | tf_op jit(solution)/shard_map/ppermute | solution.py:16
  64.4 14.8 %collective-permute-start.2 = (bf16[256,640]{1,0:T(8,128)(2,1)S(1)}, bf16[256,640]{1,0:T(8,128)(2,1)}, u32[]{:S(2)}, u32[]{:S(2)}) collective-permute-start(bf16[256,640]{1,0:T(8,128)(2,1)S(1)} %copy-done.12), channel_id=1, source_target_pairs={{65,0},{66,1},{67,2},{68,3},{69,4},{70,5},{71,6},{72,7},{73,8},{74... | collective-permute-start | bytes 983048 | tf_op jit(solution)/shard_map/ppermute | solution.py:16
  84.2 10.9 %copy-start.14 = (f32[10,512]{1,0:T(8,128)S(1)}, f32[10,512]{1,0:T(8,128)}, u32[]{:S(2)}) copy-start(f32[10,512]{1,0:T(8,128)} %get-tuple-element.27) | copy-start | bytes 61444
  84.2 11.0 %copy-start.6 = (f32[10,64,512]{2,1,0:T(8,128)S(1)}, f32[10,64,512]{2,1,0:T(8,128)}, u32[]{:S(2)}) copy-start(f32[10,64,512]{2,1,0:T(8,128)} %fusion.7) | copy-start | bytes 3932164
  84.2 11.0 %copy-start.7 = (bf16[1024,640]{0,1:T(8,128)(2,1)S(1)}, bf16[1024,640]{0,1:T(8,128)(2,1)}, u32[]{:S(2)}) copy-start(bf16[1024,640]{0,1:T(8,128)(2,1)} %copy.29) | copy-start | bytes 3932164
  95.1 9.0 %copy-start.18 = (bf16[640,1280]{1,0:T(8,128)(2,1)S(1)}, bf16[640,1280]{1,0:T(8,128)(2,1)}, u32[]{:S(2)}) copy-start(bf16[640,1280]{1,0:T(8,128)(2,1)} %param.17) | copy-start | bytes 4915204
  108.8 9.6 %collective-permute-start.10 = (bf16[256,640]{1,0:T(8,128)(2,1)}, bf16[256,640]{1,0:T(8,128)(2,1)}, u32[]{:S(2)}, u32[]{:S(2)}) collective-permute-start(bf16[256,640]{1,0:T(8,128)(2,1)} %get-tuple-element.12), channel_id=1, source_target_pairs={{96,0},{97,1},{98,2},{99,3},{100,4},{101,5},{102,6},{103,7},{104,8... | collective-permute-start | bytes 983048 | tf_op jit(solution)/shard_map/ppermute | solution.py:16
  109.8 11.8 %collective-permute-start.8 = (bf16[256,640]{1,0:T(8,128)(2,1)}, bf16[256,640]{1,0:T(8,128)(2,1)}, u32[]{:S(2)}, u32[]{:S(2)}) collective-permute-start(bf16[256,640]{1,0:T(8,128)(2,1)} %get-tuple-element.14), channel_id=1, source_target_pairs={{96,0},{97,1},{98,2},{99,3},{100,4},{101,5},{102,6},{103,7},{104,8... | collective-permute-start | bytes 983048 | tf_op jit(solution)/shard_map/ppermute | solution.py:16
  112.9 9.8 %collective-permute-start.11 = (bf16[256,640]{1,0:T(8,128)(2,1)S(1)}, bf16[256,640]{1,0:T(8,128)(2,1)}, u32[]{:S(2)}, u32[]{:S(2)}) collective-permute-start(bf16[256,640]{1,0:T(8,128)(2,1)S(1)} %get-tuple-element.11), channel_id=1, source_target_pairs={{32,0},{33,1},{34,2},{35,3},{36,4},{37,5},{38,6},{39,7},{40,8},{41... | collective-permute-start | bytes 983048 | tf_op jit(solution)/shard_map/ppermute | solution.py:16
  112.9 14.8 %collective-permute-start.9 = (bf16[256,640]{1,0:T(8,128)(2,1)S(1)}, bf16[256,640]{1,0:T(8,128)(2,1)}, u32[]{:S(2)}, u32[]{:S(2)}) collective-permute-start(bf16[256,640]{1,0:T(8,128)(2,1)S(1)} %get-tuple-element.13), channel_id=1, source_target_pairs={{32,0},{33,1},{34,2},{35,3},{36,4},{37,5},{38,6},{39,7},{40,8},{41... | collective-permute-start | bytes 983048 | tf_op jit(solution)/shard_map/ppermute | solution.py:16
  123.7 71.5 %copy-start.11 = (bf16[2,256,640]{2,1,0:T(8,128)(2,1)}, bf16[2,256,640]{2,1,0:T(8,128)(2,1)S(1)}, u32[]{:S(2)}) copy-start(bf16[2,256,640]{2,1,0:T(8,128)(2,1)S(1)} %bitcast_dynamic-update-slice_fusion) | copy-start | bytes 1966084
  123.7 71.5 %copy-start.13 = (f32[1280]{0:T(1024)S(1)}, f32[1280]{0:T(1024)}, u32[]{:S(2)}) copy-start(f32[1280]{0:T(1024)} %param.19) | copy-start | bytes 15364
  (8 other events, 18.7 us)
Sparse Core Ops, SparseCore 0:
  107.0 85.9 all-reduce.1
where the time goes:
time: 206 us; the launch traced here: 205 us
  waiting for transfers between devices  73.2 us (36%)
  matrix products  39.1 us (19%)
  local copies, waits for them, and re-layouts  29.9 us (15%)
  between operations  27.5 us (13%)
  starting transfers between devices  22.1 us (11%)
  other arithmetic  13.2 us (6%)
    psum x1, waiting for transfers between devices, body(): branch = lax.psum(partial_branch, 'kv')  63.5 us
    ppermute x12, starting transfers between devices, from_behind(): return lax.ppermute(block, axis, route)  22.1 us
    dot_general x2, matrix products, attend(): jnp.einsum('qhd,khd->hqk', query_heads, key_heads, preferred_element_type...  15.6 us
    dot_general x2, matrix products, attend(): jnp.einsum('hqk,khd->qhd', weights.astype(jnp.bfloat16), value_heads, pre...  11.9 us
    ppermute x12, waiting for transfers between devices, from_behind(): return lax.ppermute(block, axis, route)  9.72 us
  transfers between devices with their start and end apart: 13, of which 4 were waited for; matrix products, arithmetic and copies ran while one was open for 21% of the time, Pallas kernels for 0%

commit v1 on v0

--- a/solution.py
+++ b/solution.py
@@ -8,6 +8,12 @@
 PAGE = 256
 PMAX = 4
 epsilon = 1e-06
+
+
+def summed_here(x, name):
+    shards = lax.all_gather(x, name, axis=0, tiled=False)
+    acc = shards.sum(axis=0)
+    return acc
 
 
 def from_behind(block, axis, distance):
@@ -125,7 +131,7 @@
     mixed = mixed + more_mixed
     attended = (mixed / totals.T[:, :, None]).astype(jnp.bfloat16).reshape(tokens_here, width_half)
     partial_branch = jnp.dot(attended, w_out, preferred_element_type=jnp.float32)
-    branch = lax.psum(partial_branch, "kv")
+    branch = summed_here(partial_branch, "kv")
     updated = anchor + eigen_rate * (rms_scale(branch) - anchor)
     layer_out = rms_scale(updated).astype(jnp.bfloat16)
     new_keys, new_values = relay(key_rows, value_rows, placement)

time: 206 us -> 198 us (0.961)
  waiting for transfers between devices: 73.2 us -> 62 us
  other arithmetic: 13.2 us -> 17.8 us
    psum x1 -> x0, waiting for transfers between devices: 63.5 us -> none  [body(): branch = lax.psum(partial_branch, 'kv')]
    all_gather x0 -> x1, waiting for transfers between devices: none -> 52 us  [summed_here(): shards = lax.all_gather(x, name, axis=0, tiled=False)]
    reduce_sum x0 -> x1, other arithmetic: none -> 4.59 us  [summed_here(): acc = shards.sum(axis=0)]
  transfers between devices with their start and end apart: 13 -> 13, of which waited for: 4 -> 4; matrix products, arithmetic and copies ran while one was open for 21% -> 22% of each run, Pallas kernels for 0% -> 0%
where the time goes in v1:
time: 198 us; the launch traced here: 197 us
  waiting for transfers between devices  62 us (31%)
  matrix products  39 us (20%)
  local copies, waits for them, and re-layouts  29.1 us (15%)
  between operations  27.2 us (14%)
  starting transfers between devices  22.1 us (11%)
  other arithmetic  17.8 us (9%)
    all_gather x1, waiting for transfers between devices, summed_here(): shards = lax.all_gather(x, name, axis=0, tiled=False)  52 us
    ppermute x12, starting transfers between devices, from_behind(): return lax.ppermute(block, axis, route)  22.1 us
    dot_general x2, matrix products, attend(): jnp.einsum('qhd,khd->hqk', query_heads, key_heads, preferred_element_type...  15.6 us
    dot_general x2, matrix products, attend(): jnp.einsum('hqk,khd->qhd', weights.astype(jnp.bfloat16), value_heads, pre...  11.9 us
    ppermute x12, waiting for transfers between devices, from_behind(): return lax.ppermute(block, axis, route)  10 us
    reduce_sum x1, other arithmetic, summed_here(): acc = shards.sum(axis=0)  4.59 us
    dot_general x1, matrix products, body(): jnp.dot(hidden_in, w_key, preferred_element_type=jnp.float32)  4.1 us
  transfers between devices with their start and end apart: 13, of which 4 were waited for; matrix products, arithmetic and copies ran while one was open for 22% of the time, Pallas kernels for 0%

profile of v1, /device:TPU:1, one launch (start us, length us, event | category | flops | bytes accessed | tf_op | source)
XLA Modules:
  0.0 197.2 jit_solution(13607699880387781058)
XLA Ops:
  16.5 2.5 %dynamic-slice_bitcast_fusion.3 = (bf16[256,640]{1,0:T(8,128)(2,1)}, bf16[256,640]{1,0:T(8,128)(2,1)}, bf16[256,640]{1,0:T(8,128)(2,1)}, bf16[256,640]{1,0:T(8,128)(2,1)}) fusion(bf16[4,256,640]{2,1,0:T(8,128)(2,1)} %param.20, s32[]{:T(128)S(6)} %select_n.116, s32[]{:T(128)S(6)} %select_n.120, s32[]{:T(128)S(6)} %select_n.128, s32[]{:T(128)S(6)} %select_n.124), kind=kLoop, calls=%fused_computation.39 | loop fusion | bytes 2621456 | tf_op jit(solution)/shard_map/jit(dynamic_index_in_dim)/squeeze | solution.py:58
  19.0 3.2 %collective-permute-start.4 = (bf16[256,640]{1,0:T(8,128)(2,1)}, bf16[256,640]{1,0:T(8,128)(2,1)S(1)}, u32[]{:S(2)}, u32[]{:S(2)}) collective-permute-start(bf16[256,640]{1,0:T(8,128)(2,1)} %get-tuple-element.3), channel_id=1, source_target_pairs={{1,0},{2,1},{3,2},{4,3},{5,4},{6,5},{7,6},{8,7},{9,8},{10,9},{11,1... | collective-permute-start | bytes 983048 | tf_op jit(solution)/shard_map/ppermute | solution.py:22
  22.3 7.2 %collective-permute-start.5 = (bf16[256,640]{1,0:T(8,128)(2,1)}, bf16[256,640]{1,0:T(8,128)(2,1)}, u32[]{:S(2)}, u32[]{:S(2)}) collective-permute-start(bf16[256,640]{1,0:T(8,128)(2,1)} %get-tuple-element.4), channel_id=1, source_target_pairs={{33,0},{34,1},{35,2},{36,3},{37,4},{38,5},{39,6},{40,7},{41,8},{42... | collective-permute-start | bytes 983048 | tf_op jit(solution)/shard_map/ppermute | solution.py:22
  35.0 2.2 %copy.21 = bf16[512,640]{0,1:T(8,128)(2,1)} copy(bf16[512,640]{1,0:T(8,128)(2,1)} %fusion.22) | data formatting | bytes 1310720 | tf_op jit(solution)/shard_map/convert_element_type | solution.py:111
  37.2 2.7 %fusion.38 = (f32[512,640]{1,0:T(8,128)}, f32[512,640]{1,0:T(8,128)}) fusion(bf16[512,1280]{1,0:T(8,128)(2,1)S(1)} %copy-done.3, bf16[1280,640]{1,0:T(8,128)(2,1)S(1)} %copy-done), kind=kOutput, calls=%fused_computation.71 | convolution fusion | flops 839188480 | bytes 5570560 | tf_op jit(solution)/shard_map/dot_general | solution.py:106
  43.4 4.1 %fusion.37 = (f32[512,640]{1,0:T(8,128)}, f32[512,640]{1,0:T(8,128)}) fusion(bf16[512,1280]{1,0:T(8,128)(2,1)S(1)} %copy-done.3, bf16[1280,640]{1,0:T(8,128)(2,1)} %param.15), kind=kOutput, calls=%fused_computation.70 | convolution fusion | flops 839188480 | bytes 5570560 | tf_op jit(solution)/shard_map/dot_general | solution.py:108
  51.0 2.8 %multiply_convert_fusion.1 = (bf16[512,640]{1,0:T(8,128)(2,1)S(1)}, bf16[512,640]{1,0:T(8,128)(2,1)S(1)}) fusion(f32[512,640]{1,0:T(8,128)} %get-tuple-element.24, f32[512,640]{1,0:T(8,128)} %copy.26, f32[640]{0:T(1024)S(1)} %copy-done.15, f32[512,640]{1,0:T(8,128)} %get-tuple-element.26, f32[512,640]{1,0:T(8,128)} %copy.23), kind=kLoop, calls=%fused_computation.28 | loop fusion | flops 1966080 | bytes 6556160 | tf_op jit(solution)/shard_map/convert_element_type | solution.py:32
  56.0 4.7 %fusion.5 = (f32[10,512]{1,0:T(8,128)}, f32[10,512,512]{1,2,0:T(8,128)S(1)}) fusion(pred[512,512]{0,1:T(8,128)(4,1)S(1)} %fusion.23, bf16[512,10,64]{0,2,1:T(8,128)(2,1)} %bitcast.73, bf16[512,10,64]{0,2,1:T(8,128)(2,1)} %bitcast.75), kind=kOutput, calls=%fused_computation.6 | convolution fusion | flops 343403520 | bytes 12079104 | tf_op jit(solution)/shard_map/qhd,khd->hqk/dot_general | solution.py:38
  60.7 2.8 %collective-permute-start.1 = (bf16[256,640]{1,0:T(8,128)(2,1)}, bf16[256,640]{1,0:T(8,128)(2,1)}, u32[]{:S(2)}, u32[]{:S(2)}) collective-permute-start(bf16[256,640]{1,0:T(8,128)(2,1)} %get-tuple-element.8), channel_id=1, source_target_pairs={{33,0},{34,1},{35,2},{36,3},{37,4},{38,5},{39,6},{40,7},{41,8},{42... | collective-permute-start | bytes 983048 | tf_op jit(solution)/shard_map/ppermute | solution.py:22
  64.4 2.7 %collective-permute-start.2 = (bf16[256,640]{1,0:T(8,128)(2,1)S(1)}, bf16[256,640]{1,0:T(8,128)(2,1)}, u32[]{:S(2)}, u32[]{:S(2)}) collective-permute-start(bf16[256,640]{1,0:T(8,128)(2,1)S(1)} %copy-done.12), channel_id=1, source_target_pairs={{65,0},{66,1},{67,2},{68,3},{69,4},{70,5},{71,6},{72,7},{73,8},{74... | collective-permute-start | bytes 983048 | tf_op jit(solution)/shard_map/ppermute | solution.py:22
  67.0 2.9 %fusion.7 = f32[10,64,512]{2,1,0:T(8,128)} fusion(bf16[512,10,64]{0,2,1:T(8,128)(2,1)S(1)} %bitcast.70, f32[10,512,512]{1,2,0:T(8,128)S(1)} %get-tuple-element.28, pred[512,512]{0,1:T(8,128)(4,1)S(1)} %fusion.23), kind=kOutput, calls=%fused_computation.8 | convolution fusion | flops 343408640 | bytes 12713984 | tf_op jit(solution)/shard_map/hqk,khd->qhd/dot_general | solution.py:43
  70.6 2.4 %pad_maximum_fusion.1 = bf16[1024,640]{1,0:T(8,128)(2,1)} fusion(bf16[256,640]{1,0:T(8,128)(2,1)} %collective-permute-done.7, bf16[256,640]{1,0:T(8,128)(2,1)} %collective-permute-done.6, bf16[256,640]{1,0:T(8,128)(2,1)} %collective-permute-done.5, bf16[256,640]{1,0:T(8,128)(2,1)S(1)} %collective-permute-done.4), kind=kLoop, calls=%fused_computation.26 | loop fusion | flops 5242880 | bytes 2621440 | tf_op jit(solution)/shard_map/concatenate | solution.py:125
  73.0 2.5 %copy.30 = bf16[1024,640]{0,1:T(8,128)(2,1)} copy(bf16[1024,640]{1,0:T(8,128)(2,1)} %pad_maximum_fusion.1) | data formatting | bytes 2621440 | tf_op jit(solution)/shard_map/concatenate | solution.py:125
  75.5 3.6 %collective-permute-done.2 = bf16[256,640]{1,0:T(8,128)(2,1)} collective-permute-done((bf16[256,640]{1,0:T(8,128)(2,1)S(1)}, bf16[256,640]{1,0:T(8,128)(2,1)}, u32[]{:S(2)}, u32[]{:S(2)}) %collective-permute-start.2) | collective-permute-done | bytes 327712 | tf_op jit(solution)/shard_map/ppermute | solution.py:22
  79.1 2.5 %pad_maximum_fusion = bf16[1024,640]{1,0:T(8,128)(2,1)} fusion(bf16[256,640]{1,0:T(8,128)(2,1)} %collective-permute-done.3, bf16[256,640]{1,0:T(8,128)(2,1)} %collective-permute-done.2, bf16[256,640]{1,0:T(8,128)(2,1)} %collective-permute-done.1, bf16[256,640]{1,0:T(8,128)(2,1)} %collective-permute-done), kind=kLoop, calls=%fused_computation.25 | loop fusion | flops 5242880 | bytes 2621440 | tf_op jit(solution)/shard_map/concatenate | solution.py:126
  81.6 2.6 %copy.29 = bf16[1024,640]{0,1:T(8,128)(2,1)} copy(bf16[1024,640]{1,0:T(8,128)(2,1)} %pad_maximum_fusion) | data formatting | bytes 2621440 | tf_op jit(solution)/shard_map/concatenate | solution.py:126
  84.2 10.9 %fusion = (f32[10,512]{1,0:T(8,128)S(1)}, f32[10,512,1024]{2,1,0:T(8,128)}) fusion(pred[1024]{0:T(1024)(128)(4,1)S(1)} %fusion.26, bf16[512,10,64]{0,2,1:T(8,128)(2,1)S(1)} %bitcast.74, bf16[1024,10,64]{0,2,1:T(8,128)(2,1)} %bitcast.71), kind=kOutput, calls=%fused_computation.1 | convolution fusion | flops 686812160 | bytes 22959104 | tf_op jit(solution)/shard_map/qhd,khd->hqk/dot_general | solution.py:38
  95.1 9.0 %divide_convert_fusion = bf16[512,10,64]{0,2,1:T(8,128)(2,1)S(1)} fusion(f32[10,64,512]{2,1,0:T(8,128)S(1)} %copy-done.6, bf16[1024,10,64]{0,2,1:T(8,128)(2,1)S(1)} %bitcast.72, f32[10,512,1024]{2,1,0:T(8,128)} %get-tuple-element.30, pred[1024]{0:T(1024)(128)(4,1)S(1)} %fusion.26, f32[512,10]{0,1:T(8,128)S(1)} %add_bitcast_fusion), kind=kOutput, calls=%fused_computation.27 | convolution fusion | flops 687800320 | bytes 24269824 | tf_op jit(solution)/shard_map/hqk,khd->qhd/dot_general | solution.py:43
  104.2 2.7 %fusion.39 = f32[512,1280]{1,0:T(8,128)} fusion(bf16[512,640]{0,1:T(8,128)(2,1)S(1)} %bitcast.76, bf16[640,1280]{1,0:T(8,128)(2,1)S(1)} %copy-done.18), kind=kOutput, calls=%fused_computation.72 | convolution fusion | flops 838860800 | bytes 4915200 | tf_op jit(solution)/shard_map/dot_general | solution.py:133
  109.8 3.1 %collective-permute-start.8 = (bf16[256,640]{1,0:T(8,128)(2,1)}, bf16[256,640]{1,0:T(8,128)(2,1)}, u32[]{:S(2)}, u32[]{:S(2)}) collective-permute-start(bf16[256,640]{1,0:T(8,128)(2,1)} %get-tuple-element.14), channel_id=1, source_target_pairs={{96,0},{97,1},{98,2},{99,3},{100,4},{101,5},{102,6},{103,7},{104,8... | collective-permute-start | bytes 983048 | tf_op jit(solution)/shard_map/ppermute | solution.py:22
  119.1 2.5 %collective-permute-done.8 = bf16[256,640]{1,0:T(8,128)(2,1)} collective-permute-done((bf16[256,640]{1,0:T(8,128)(2,1)}, bf16[256,640]{1,0:T(8,128)(2,1)}, u32[]{:S(2)}, u32[]{:S(2)}) %collective-permute-start.8) | collective-permute-done | bytes 327712 | tf_op jit(solution)/shard_map/ppermute | solution.py:22
  123.7 3.9 %collective-permute-done.9 = bf16[256,640]{1,0:T(8,128)(2,1)} collective-permute-done((bf16[256,640]{1,0:T(8,128)(2,1)S(1)}, bf16[256,640]{1,0:T(8,128)(2,1)}, u32[]{:S(2)}, u32[]{:S(2)}) %collective-permute-start.9) | collective-permute-done | bytes 327712 | tf_op jit(solution)/shard_map/ppermute | solution.py:22
  128.6 52.0 %all-gather.3.cloned.1.call-done = f32[1024,1280]{1,0:T(8,128)} async-done(((f32[512,1280]{1,0:T(8,128)}), f32[1024,1280]{1,0:T(8,128)}) %all-gather.3.cloned.1.call-update) | async-done | bytes 5242896 | tf_op jit(solution)/shard_map/all_gather | solution.py:14
  180.6 4.6 %reduce_sum.77 = f32[512,1280]{1,0:T(8,128)} reduce(f32[2,512,1280]{2,1,0:T(8,128)} %bitcast.69, f32[]{:T(128)} %constant.136.clone.1), dimensions={0}, to_apply=%region_5.6 | reduce | flops 655360 | bytes 7864324 | tf_op jit(solution)/shard_map/reduce_sum | solution.py:15
  (91 shorter events, 30.1 us)
Async XLA Ops:
  7.2 30.0 %copy-start = (bf16[1280,640]{1,0:T(8,128)(2,1)S(1)}, bf16[1280,640]{1,0:T(8,128)(2,1)}, u32[]{:S(2)}) copy-start(bf16[1280,640]{1,0:T(8,128)(2,1)} %param.14) | copy-start | bytes 4915204
  7.2 173.4 %all-gather.3.cloned.1.call-start = ((), (), s32[]{:S(2)}) async-start(), calls=%async_computation | async-start | bytes 7864320 | tf_op jit(solution)/shard_map/all_gather | solution.py:14
  16.5 14.2 %copy-start.8 = (bf16[4,256,640]{2,1,0:T(8,128)(2,1)S(1)}, bf16[4,256,640]{2,1,0:T(8,128)(2,1)}, u32[]{:S(2)}) copy-start(bf16[4,256,640]{2,1,0:T(8,128)(2,1)} %param.21) | copy-start | bytes 3932164
  19.0 13.5 %copy-start.3 = (bf16[512,1280]{1,0:T(8,128)(2,1)S(1)}, bf16[512,1280]{1,0:T(8,128)(2,1)}, u32[]{:S(2)}) copy-start(bf16[512,1280]{1,0:T(8,128)(2,1)} %param.13) | copy-start | bytes 3932164
  19.0 41.7 %collective-permute-start.4 = (bf16[256,640]{1,0:T(8,128)(2,1)}, bf16[256,640]{1,0:T(8,128)(2,1)S(1)}, u32[]{:S(2)}, u32[]{:S(2)}) collective-permute-start(bf16[256,640]{1,0:T(8,128)(2,1)} %get-tuple-element.3), channel_id=1, source_target_pairs={{1,0},{2,1},{3,2},{4,3},{5,4},{6,5},{7,6},{8,7},{9,8},{10,9},{11,1... | collective-permute-start | bytes 983048 | tf_op jit(solution)/shard_map/ppermute | solution.py:22
  22.3 41.3 %collective-permute-start.5 = (bf16[256,640]{1,0:T(8,128)(2,1)}, bf16[256,640]{1,0:T(8,128)(2,1)}, u32[]{:S(2)}, u32[]{:S(2)}) collective-permute-start(bf16[256,640]{1,0:T(8,128)(2,1)} %get-tuple-element.4), channel_id=1, source_target_pairs={{33,0},{34,1},{35,2},{36,3},{37,4},{38,5},{39,6},{40,7},{41,8},{42... | collective-permute-start | bytes 983048 | tf_op jit(solution)/shard_map/ppermute | solution.py:22
  29.5 34.9 %collective-permute-start.7 = (bf16[256,640]{1,0:T(8,128)(2,1)}, bf16[256,640]{1,0:T(8,128)(2,1)}, u32[]{:S(2)}, u32[]{:S(2)}) collective-permute-start(bf16[256,640]{1,0:T(8,128)(2,1)} %get-tuple-element.5), channel_id=1, source_target_pairs={{97,0},{98,1},{99,2},{100,3},{101,4},{102,5},{103,6},{104,7},{105,... | collective-permute-start | bytes 983048 | tf_op jit(solution)/shard_map/ppermute | solution.py:22
  30.2 40.4 %collective-permute-start.6 = (bf16[256,640]{1,0:T(8,128)(2,1)}, bf16[256,640]{1,0:T(8,128)(2,1)}, u32[]{:S(2)}, u32[]{:S(2)}) collective-permute-start(bf16[256,640]{1,0:T(8,128)(2,1)} %get-tuple-element.6), channel_id=1, source_target_pairs={{65,0},{66,1},{67,2},{68,3},{69,4},{70,5},{71,6},{72,7},{73,8},{74... | collective-permute-start | bytes 983048 | tf_op jit(solution)/shard_map/ppermute | solution.py:22
  31.8 43.7 %collective-permute-start = (bf16[256,640]{1,0:T(8,128)(2,1)}, bf16[256,640]{1,0:T(8,128)(2,1)}, u32[]{:S(2)}, u32[]{:S(2)}) collective-permute-start(bf16[256,640]{1,0:T(8,128)(2,1)} %get-tuple-element.7), channel_id=1, source_target_pairs={{1,0},{2,1},{3,2},{4,3},{5,4},{6,5},{7,6},{8,7},{9,8},{10,9},{11,1... | collective-permute-start | bytes 983048 | tf_op jit(solution)/shard_map/ppermute | solution.py:22
  56.0 8.3 %copy-start.12 = (bf16[256,640]{1,0:T(8,128)(2,1)S(1)}, bf16[256,640]{1,0:T(8,128)(2,1)}, u32[]{:S(2)}) copy-start(bf16[256,640]{1,0:T(8,128)(2,1)} %get-tuple-element.10) | copy-start | bytes 983044
  56.0 11.0 %copy-start.4 = (bf16[512,640]{0,1:T(8,128)(2,1)S(1)}, bf16[512,640]{0,1:T(8,128)(2,1)}, u32[]{:S(2)}) copy-start(bf16[512,640]{0,1:T(8,128)(2,1)} %copy.21) | copy-start | bytes 1966084
  60.7 14.7 %collective-permute-start.1 = (bf16[256,640]{1,0:T(8,128)(2,1)}, bf16[256,640]{1,0:T(8,128)(2,1)}, u32[]{:S(2)}, u32[]{:S(2)}) collective-permute-start(bf16[256,640]{1,0:T(8,128)(2,1)} %get-tuple-element.8), channel_id=1, source_target_pairs={{33,0},{34,1},{35,2},{36,3},{37,4},{38,5},{39,6},{40,7},{41,8},{42... | collective-permute-start | bytes 983048 | tf_op jit(solution)/shard_map/ppermute | solution.py:22
  63.6 11.9 %collective-permute-start.3 = (bf16[256,640]{1,0:T(8,128)(2,1)}, bf16[256,640]{1,0:T(8,128)(2,1)}, u32[]{:S(2)}, u32[]{:S(2)}) collective-permute-start(bf16[256,640]{1,0:T(8,128)(2,1)} %get-tuple-element.9), channel_id=1, source_target_pairs={{97,0},{98,1},{99,2},{100,3},{101,4},{102,5},{103,6},{104,7},{105,... | collective-permute-start | bytes 983048 | tf_op jit(solution)/shard_map/ppermute | solution.py:22
  64.4 14.8 %collective-permute-start.2 = (bf16[256,640]{1,0:T(8,128)(2,1)S(1)}, bf16[256,640]{1,0:T(8,128)(2,1)}, u32[]{:S(2)}, u32[]{:S(2)}) collective-permute-start(bf16[256,640]{1,0:T(8,128)(2,1)S(1)} %copy-done.12), channel_id=1, source_target_pairs={{65,0},{66,1},{67,2},{68,3},{69,4},{70,5},{71,6},{72,7},{73,8},{74... | collective-permute-start | bytes 983048 | tf_op jit(solution)/shard_map/ppermute | solution.py:22
  84.2 10.9 %copy-start.14 = (f32[10,512]{1,0:T(8,128)S(1)}, f32[10,512]{1,0:T(8,128)}, u32[]{:S(2)}) copy-start(f32[10,512]{1,0:T(8,128)} %get-tuple-element.27) | copy-start | bytes 61444
  84.2 11.0 %copy-start.6 = (f32[10,64,512]{2,1,0:T(8,128)S(1)}, f32[10,64,512]{2,1,0:T(8,128)}, u32[]{:S(2)}) copy-start(f32[10,64,512]{2,1,0:T(8,128)} %fusion.7) | copy-start | bytes 3932164
  84.2 11.0 %copy-start.7 = (bf16[1024,640]{0,1:T(8,128)(2,1)S(1)}, bf16[1024,640]{0,1:T(8,128)(2,1)}, u32[]{:S(2)}) copy-start(bf16[1024,640]{0,1:T(8,128)(2,1)} %copy.29) | copy-start | bytes 3932164
  95.1 9.0 %copy-start.18 = (bf16[640,1280]{1,0:T(8,128)(2,1)S(1)}, bf16[640,1280]{1,0:T(8,128)(2,1)}, u32[]{:S(2)}) copy-start(bf16[640,1280]{1,0:T(8,128)(2,1)} %param.17) | copy-start | bytes 4915204
  108.7 9.2 %collective-permute-start.10 = (bf16[256,640]{1,0:T(8,128)(2,1)}, bf16[256,640]{1,0:T(8,128)(2,1)}, u32[]{:S(2)}, u32[]{:S(2)}) collective-permute-start(bf16[256,640]{1,0:T(8,128)(2,1)} %get-tuple-element.12), channel_id=1, source_target_pairs={{96,0},{97,1},{98,2},{99,3},{100,4},{101,5},{102,6},{103,7},{104,8... | collective-permute-start | bytes 983048 | tf_op jit(solution)/shard_map/ppermute | solution.py:22
  109.8 11.8 %collective-permute-start.8 = (bf16[256,640]{1,0:T(8,128)(2,1)}, bf16[256,640]{1,0:T(8,128)(2,1)}, u32[]{:S(2)}, u32[]{:S(2)}) collective-permute-start(bf16[256,640]{1,0:T(8,128)(2,1)} %get-tuple-element.14), channel_id=1, source_target_pairs={{96,0},{97,1},{98,2},{99,3},{100,4},{101,5},{102,6},{103,7},{104,8... | collective-permute-start | bytes 983048 | tf_op jit(solution)/shard_map/ppermute | solution.py:22
  112.8 9.8 %collective-permute-start.11 = (bf16[256,640]{1,0:T(8,128)(2,1)S(1)}, bf16[256,640]{1,0:T(8,128)(2,1)}, u32[]{:S(2)}, u32[]{:S(2)}) collective-permute-start(bf16[256,640]{1,0:T(8,128)(2,1)S(1)} %get-tuple-element.11), channel_id=1, source_target_pairs={{32,0},{33,1},{34,2},{35,3},{36,4},{37,5},{38,6},{39,7},{40,8},{41... | collective-permute-start | bytes 983048 | tf_op jit(solution)/shard_map/ppermute | solution.py:22
  112.8 14.8 %collective-permute-start.9 = (bf16[256,640]{1,0:T(8,128)(2,1)S(1)}, bf16[256,640]{1,0:T(8,128)(2,1)}, u32[]{:S(2)}, u32[]{:S(2)}) collective-permute-start(bf16[256,640]{1,0:T(8,128)(2,1)S(1)} %get-tuple-element.13), channel_id=1, source_target_pairs={{32,0},{33,1},{34,2},{35,3},{36,4},{37,5},{38,6},{39,7},{40,8},{41... | collective-permute-start | bytes 983048 | tf_op jit(solution)/shard_map/ppermute | solution.py:22
  123.7 61.5 %copy-start.11 = (bf16[2,256,640]{2,1,0:T(8,128)(2,1)}, bf16[2,256,640]{2,1,0:T(8,128)(2,1)S(1)}, u32[]{:S(2)}) copy-start(bf16[2,256,640]{2,1,0:T(8,128)(2,1)S(1)} %bitcast_dynamic-update-slice_fusion) | copy-start | bytes 1966084
  128.6 56.6 %copy-start.10 = (bf16[2,256,640]{2,1,0:T(8,128)(2,1)}, bf16[2,256,640]{2,1,0:T(8,128)(2,1)S(1)}, u32[]{:S(2)}) copy-start(bf16[2,256,640]{2,1,0:T(8,128)(2,1)S(1)} %bitcast_dynamic-update-slice_fusion.2) | copy-start | bytes 1966084
  (8 other events, 24.8 us)
Sparse Core Ops, SparseCore 0:
  107.0 73.5 all-gather.2
